TPU v7x, 32 devices: a whole 2x2x4 slice. The times are simulated.
32 devices in a mesh: tp: 4 (over y, core), dp: 8 (over z, x).
Axes of the slice: x: 2, y: 2, z: 4, core: 2. Of those that a mesh axis runs over, the one named last changes fastest.
Arguments:
- tokens: bfloat16 [24, 1024, 768], P('dp', 'tp'), may hold values from -6 to 6
- lengths: int32 [24], P('dp'), may hold values from 196 to 1024, as said below
- ln_gain: float32 [768], replicated, may hold values from 0.1 to 1.9
- w_qkv: bfloat16 [768, 2304], P(None, 'tp'), may hold values from -0.21875 to 0.21875
- q_gain: float32 [12, 64], P('tp'), may hold values from 0.1 to 1.9
- k_gain: float32 [12, 64], P('tp'), may hold values from 0.1 to 1.9
- w_proj: bfloat16 [768, 768], P('tp'), may hold values from -1.75 to 1.75
- w_fc1: bfloat16 [768, 3072], P(None, 'tp'), may hold values from -0.21875 to 0.21875
- b_fc1: float32 [3072], P('tp'), may hold values from -3 to 3
- w_fc2: bfloat16 [3072, 768], P('tp'), may hold values from -0.109375 to 0.109375
- b_fc2: float32 [768], replicated, may hold values from -2 to 2
- d_out: bfloat16 [24, 1024, 768], P('dp', 'tp'), may hold values from -6 to 6
Outputs:
- output: bfloat16 [24, 1024, 768], P('dp', 'tp')
- d_tokens: float32 [24, 1024, 768], P('dp', 'tp')
- d_ln_gain: float32 [768], replicated
- d_qkv: float32 [768, 2304], P(None, 'tp')
- d_q_gain: float32 [12, 64], P('tp')
- d_k_gain: float32 [12, 64], P('tp')
- d_proj: float32 [768, 768], P('tp')
- d_fc1: float32 [768, 3072], P(None, 'tp')
- d_bias_one: float32 [3072], P('tp')
- d_fc2: float32 [3072, 768], P('tp')
- d_bias_two: float32 [768], replicated
Inputs may be any that keep to these rules, and one draw needn't show every extreme that they name: `lengths`: each image's length is one of 196, 576 and 1024; every draw holds all three.
All inputs are finite; a program needn't handle non-finite values.
Results may differ from a plain program's by a relative error of at most 0.014.
Values may be sent and summed in bfloat16 or wider, within the bound.
No kernel may reach another device: no remote copies, remote signals or barrier semaphores. Data moves between devices by JAX's collectives and lax.ppermute only.
A program may use at most 192 MiB of HBM per device.

v0:
```python
import jax
import jax.numpy as jnp
from jax import lax
from jax.sharding import PartitionSpec as P

epsilon = 1e-06
masked_value = -1e30


def layer_norm(values, scale_gain):
    average = jnp.mean(values, axis=-1, keepdims=True)
    centred = values - average
    variance = jnp.mean(centred * centred, axis=-1, keepdims=True)
    return centred * lax.rsqrt(variance + epsilon) * scale_gain


def gelu_exact(values):
    return jax.nn.gelu(values, approximate=False)


def score_block(queries, keys_normed, length, factor):
    scores = (
        jnp.einsum("qhd,khd->hqk", queries, keys_normed, preferred_element_type=jnp.float32)
        * factor
    )
    visible = lax.broadcasted_iota(jnp.int32, scores.shape, 2) < length
    return (scores, visible)


def forward_keys(factor, operands):
    queries, keys_normed, value_rows, length = operands
    scores, visible = score_block(queries, keys_normed, length, factor)
    masked = jnp.where(visible, scores, masked_value)
    row_peak = jnp.max(masked, axis=-1, keepdims=True)
    exponent = jnp.exp(masked - row_peak)
    row_total = jnp.sum(exponent, axis=-1, keepdims=True)
    probability = (exponent / row_total).astype(jnp.bfloat16)
    attended = jnp.einsum(
        "hqk,khd->qhd", probability, value_rows, preferred_element_type=jnp.float32
    )
    return (attended, row_peak[..., 0] + jnp.log(row_total[..., 0]))


def backward_keys(factor, operands):
    queries, keys_normed, value_rows, d_attended, logsum, length = operands
    scores, visible = score_block(queries, keys_normed, length, factor)
    probability = jnp.where(visible, jnp.exp(scores - logsum[..., None]), 0.0)
    d_probs = jnp.einsum("qhd,khd->hqk", d_attended, value_rows, preferred_element_type=jnp.float32)
    row_dot = jnp.sum(probability * d_probs, axis=-1, keepdims=True)
    d_scores = (probability * (d_probs - row_dot)).astype(jnp.bfloat16)
    d_queries = (
        jnp.einsum("hqk,khd->qhd", d_scores, keys_normed, preferred_element_type=jnp.float32)
        * factor
    )
    d_keys = (
        jnp.einsum("hqk,qhd->khd", d_scores, queries, preferred_element_type=jnp.float32) * factor
    )
    d_values = jnp.einsum(
        "hqk,qhd->khd",
        probability.astype(jnp.bfloat16),
        d_attended,
        preferred_element_type=jnp.float32,
    )
    return (d_queries, d_keys, d_values)


def shards(
    tokens, lengths, ln_gain, w_qkv, q_gain, k_gain, w_proj, w_fc1, b_fc1, w_fc2, b_fc2, d_out
):
    images = tokens.shape[0]
    heads_here = q_gain.shape[0]
    head_size = q_gain.shape[1]
    factor = head_size ** (-0.5)
    tokens_float = tokens.astype(jnp.float32)
    normed_local = layer_norm(tokens_float, ln_gain).astype(jnp.bfloat16)
    normed = lax.all_gather(normed_local, "tp", axis=1, tiled=True)
    seq_len = normed.shape[1]
    joined = jnp.einsum("bsd,dc->bsc", normed, w_qkv, preferred_element_type=jnp.float32)
    split_heads = joined.reshape(images, seq_len, heads_here, 3, head_size)
    query_raw = split_heads[:, :, :, 0]
    key_raw = split_heads[:, :, :, 1]
    queries = layer_norm(query_raw, q_gain).astype(jnp.bfloat16)
    keys_normed = layer_norm(key_raw, k_gain).astype(jnp.bfloat16)
    value_rows = split_heads[:, :, :, 2].astype(jnp.bfloat16)

    def attend_image(operands):
        return forward_keys(factor, operands)

    attended, logsum = lax.map(attend_image, (queries, keys_normed, value_rows, lengths))
    attended = attended.reshape(images, seq_len, heads_here * head_size).astype(jnp.bfloat16)
    hidden = jnp.einsum("bsd,df->bsf", normed, w_fc1, preferred_element_type=jnp.float32) + b_fc1
    active = gelu_exact(hidden).astype(jnp.bfloat16)
    partial_sum = jnp.einsum("bsc,cd->bsd", attended, w_proj, preferred_element_type=jnp.float32)
    partial_sum = partial_sum + jnp.einsum(
        "bsf,fd->bsd", active, w_fc2, preferred_element_type=jnp.float32
    )
    summed = lax.psum_scatter(
        partial_sum.astype(jnp.bfloat16), "tp", scatter_dimension=1, tiled=True
    ).astype(jnp.float32)
    output = (tokens_float + summed + b_fc2).astype(jnp.bfloat16)
    d_rows = lax.all_gather(d_out, "tp", axis=1, tiled=True)
    d_fc2 = jnp.einsum("bsf,bsd->fd", active, d_rows, preferred_element_type=jnp.float32)
    d_proj = jnp.einsum("bsc,bsd->cd", attended, d_rows, preferred_element_type=jnp.float32)
    d_active = jnp.einsum("bsd,fd->bsf", d_rows, w_fc2, preferred_element_type=jnp.float32)
    _, gelu_back = jax.vjp(gelu_exact, hidden)
    d_hidden = gelu_back(d_active)[0].astype(jnp.bfloat16)
    d_fc1 = jnp.einsum("bsd,bsf->df", normed, d_hidden, preferred_element_type=jnp.float32)
    d_bias_one = jnp.sum(d_hidden, axis=(0, 1), dtype=jnp.float32)
    d_normed = jnp.einsum("bsf,df->bsd", d_hidden, w_fc1, preferred_element_type=jnp.float32)
    d_attended = jnp.einsum(
        "bsd,cd->bsc", d_rows, w_proj, preferred_element_type=jnp.float32
    ).astype(jnp.bfloat16)
    d_heads = d_attended.reshape(images, seq_len, heads_here, head_size)

    def back_image(operands):
        return backward_keys(factor, operands)

    d_queries, d_keys, d_values = lax.map(
        back_image, (queries, keys_normed, value_rows, d_heads, logsum, lengths)
    )
    _, query_back = jax.vjp(layer_norm, query_raw, q_gain)
    d_query_raw, d_q_gain = query_back(d_queries)
    _, key_back = jax.vjp(layer_norm, key_raw, k_gain)
    d_key_raw, d_k_gain = key_back(d_keys)
    d_joined = (
        jnp.stack([d_query_raw, d_key_raw, d_values], axis=3)
        .reshape(images, seq_len, -1)
        .astype(jnp.bfloat16)
    )
    d_qkv = jnp.einsum("bsd,bsc->dc", normed, d_joined, preferred_element_type=jnp.float32)
    d_normed = d_normed + jnp.einsum(
        "bsc,dc->bsd", d_joined, w_qkv, preferred_element_type=jnp.float32
    )
    d_local = lax.psum_scatter(
        d_normed.astype(jnp.bfloat16), "tp", scatter_dimension=1, tiled=True
    ).astype(jnp.float32)
    _, norm_back = jax.vjp(layer_norm, tokens_float, ln_gain)
    d_tokens_part, d_ln_gain = norm_back(d_local)
    d_tokens = d_out.astype(jnp.float32) + d_tokens_part
    d_bias_two = jnp.sum(d_out, axis=(0, 1), dtype=jnp.float32)
    d_ln_gain, d_bias_two = lax.psum((d_ln_gain, d_bias_two), ("tp", "dp"))
    d_qkv, d_q_gain, d_k_gain, d_proj, d_fc1, d_bias_one, d_fc2 = (
        lax.psum(d_qkv.astype(jnp.bfloat16), "dp").astype(jnp.float32),
        lax.psum(d_q_gain.astype(jnp.bfloat16), "dp").astype(jnp.float32),
        lax.psum(d_k_gain.astype(jnp.bfloat16), "dp").astype(jnp.float32),
        lax.psum(d_proj.astype(jnp.bfloat16), "dp").astype(jnp.float32),
        lax.psum(d_fc1.astype(jnp.bfloat16), "dp").astype(jnp.float32),
        lax.psum(d_bias_one.astype(jnp.bfloat16), "dp").astype(jnp.float32),
        lax.psum(d_fc2.astype(jnp.bfloat16), "dp").astype(jnp.float32),
    )
    return (
        output,
        d_tokens,
        d_ln_gain,
        d_qkv,
        d_q_gain,
        d_k_gain,
        d_proj,
        d_fc1,
        d_bias_one,
        d_fc2,
        d_bias_two,
    )


def solution(mesh):
    placed = (
        P("dp", "tp", None),
        P("dp"),
        P(),
        P(None, "tp"),
        P("tp", None),
        P("tp", None),
        P("tp", None),
        P(None, "tp"),
        P("tp"),
        P("tp", None),
        P(),
        P("dp", "tp", None),
    )
    return jax.shard_map(
        shards,
        mesh=mesh,
        in_specs=placed,
        out_specs=(
            P("dp", "tp", None),
            P("dp", "tp", None),
            P(),
            P(None, "tp"),
            P("tp", None),
            P("tp", None),
            P("tp", None),
            P(None, "tp"),
            P("tp"),
            P("tp", None),
            P(),
        ),
        check_vma=False,
    )
```

profile of v0, /device:TPU:0, one launch (start us, length us, event | category | flops | bytes accessed | tf_op | source)
XLA Modules:
  0.0 569.2 jit_solution(9019446906122960374)
XLA Ops:
  7.3 1.6 convert_reduce_fusion
  8.9 1.7 fusion.67
  11.9 1.4 fusion.65
  14.1 1.2 fusion.97
  15.3 2.4 copy.83
  17.7 36.0 %all-gather.3.cloned.1.call-done = bf16[3,1024,768]{2,1,0:T(8,128)(2,1)} async-done(((bf16[3,256,768]{2,1,0:T(8,128)(2,1)}), bf16[3,1024,768]{2,1,0:T(8,128)(2,1)}) %all-gather.3.cloned.1.call-update) | async-done | bytes 4718608 | tf_op jit(solution)/shard_map/all_gather | solution.py:76
  53.6 4.8 fusion.86
  59.2 1.3 fusion.77
  64.5 37.1 %while.28 = (s32[]{:T(128)}, bf16[3,1024,3,64]{1,3,2,0:T(8,128)(2,1)}, f32[3,3,1024]{2,1,0:T(4,128)}, bf16[3,1024,3,64]{1,3,2,0:T(8,128)(2,1)}, s32[3]{0:T(128)S...) while((s32[]{:T(128)}, bf16[3,1024,3,64]{1,3,2,0:T(8,128)(2,1)}, ...), condition=%wide.region_9.10_spmd.clone, body=%wide.region_6.9_spmd.sunk.clone | while | flops 843053056 | bytes 39823964 | solution.py:89
  65.8 2.4 fusion.151
  68.2 3.2 fusion.152
  72.0 4.9 fusion.153
  78.2 2.4 fusion.151
  80.5 3.2 fusion.152
  84.3 4.9 fusion.153
  90.5 2.4 fusion.151
  92.9 3.2 fusion.152
  96.7 4.9 fusion.153
  101.6 6.0 %convolution_convert_fusion = bf16[3,1024,192]{1,2,0:T(8,128)(2,1)} fusion(bf16[3,1024,768]{2,1,0:T(8,128)(2,1)} %all-gather.5.cloned.1.call-done, bf16[192,768]{1,0:T(8,128)(2,1)} %param.22), kind=kOutput, calls=%fused_computation.126 | convolution fusion | flops 906559488 | bytes 6193152 | tf_op jit(solution)/shard_map/bsd,cd->bsc/dot_general | solution.py:110
  107.6 87.6 %while.29 = (s32[]{:T(128)}, f32[3,1024,3,64]{1,3,2,0:T(8,128)}, f32[3,1024,3,64]{1,3,2,0:T(8,128)}, bf16[3,1024,3,64]{1,3,2,0:T(8,128)(2,1)}, bf16[3,1024,3,64]...) while((s32[]{:T(128)}, f32[3,1024,3,64]{1,3,2,0:T(8,128)}, ...), condition=%wide.region_13.14_spmd.clone, body=%wide.region_11.13_spmd.sunk.clone | while | flops 2060843008 | bytes 124744848 | solution.py:118
  107.8 3.1 fusion.162
  112.9 4.8 multiply_reduce_fusion.9
  117.7 5.6 multiply_convert_fusion.6
  123.3 6.0 %fusion.164 = f32[3,1024,3,64]{1,3,2,0:T(8,128)} fusion(f32[3,1024,3,64]{1,3,2,0:T(8,128)} %get-tuple-element.364, s32[]{:T(128)} %get-tuple-element.362, bf16[3,1024,1024]{1,2,0:T(8,128)(2,1)} %multiply_convert_fusion.6, bf16[3,1024,3,64]{1,3,2,0:T(8,128)(2,1)} %get-tuple-element.378), kind=kOutput, calls=%fused_computation.31.clone.1.clone | convolution fusion | flops 402849792 | bytes 7472128 | tf_op jit(solution)/shard_map/while/body/eval_jaxpr/hqk,qhd->khd/dot_general | solution.py:56
  129.3 3.1 fusion.163
  132.4 4.6 fusion.165
  137.0 2.9 fusion.162
  142.0 4.8 multiply_reduce_fusion.9
  146.8 5.6 multiply_convert_fusion.6
  152.4 6.0 %fusion.164 = f32[3,1024,3,64]{1,3,2,0:T(8,128)} fusion(f32[3,1024,3,64]{1,3,2,0:T(8,128)} %get-tuple-element.364, s32[]{:T(128)} %get-tuple-element.362, bf16[3,1024,1024]{1,2,0:T(8,128)(2,1)} %multiply_convert_fusion.6, bf16[3,1024,3,64]{1,3,2,0:T(8,128)(2,1)} %get-tuple-element.378), kind=kOutput, calls=%fused_computation.31.clone.1.clone | convolution fusion | flops 402849792 | bytes 7472128 | tf_op jit(solution)/shard_map/while/body/eval_jaxpr/hqk,qhd->khd/dot_general | solution.py:56
  158.4 3.1 fusion.163
  161.5 4.6 fusion.165
  166.1 2.9 fusion.162
  171.0 4.8 multiply_reduce_fusion.9
  175.8 5.6 multiply_convert_fusion.6
  181.5 6.0 %fusion.164 = f32[3,1024,3,64]{1,3,2,0:T(8,128)} fusion(f32[3,1024,3,64]{1,3,2,0:T(8,128)} %get-tuple-element.364, s32[]{:T(128)} %get-tuple-element.362, bf16[3,1024,1024]{1,2,0:T(8,128)(2,1)} %multiply_convert_fusion.6, bf16[3,1024,3,64]{1,3,2,0:T(8,128)(2,1)} %get-tuple-element.378), kind=kOutput, calls=%fused_computation.31.clone.1.clone | convolution fusion | flops 402849792 | bytes 7472128 | tf_op jit(solution)/shard_map/while/body/eval_jaxpr/hqk,qhd->khd/dot_general | solution.py:56
  187.5 3.1 fusion.163
  190.6 4.6 fusion.165
  195.2 2.5 multiply_reduce_fusion.4
  200.0 2.8 multiply_reduce_fusion.1
  204.4 1.9 pad_maximum_fusion
  207.1 6.4 %fusion.72 = (u8[1024,768]{1,0:T(8,128)(4,1)S(1)}, u8[1024,768]{1,0:T(8,128)(4,1)S(1)}, f32[3,1024,768]{2,1,0:T(8,128)S(1)}) fusion(f32[768]{0:T(1024)S(1)} %copy-done.43, bf16[3,1024,768]{2,1,0:T(8,128)(2,1)S(1)} %bitcast.228, bf16[768,768]{1,0:T(8,128)(2,1)S(1)} %copy-done), kind=kOutput, calls=%fused_computation.122 | convolution fusion | flops 3655335936 | bytes 16911360 | tf_op jit(solution)/shard_map/bsd,df->bsf/dot_general | solution.py:91
  213.5 23.0 %multiply_convert_fusion.1 = (bf16[3,1024,768]{2,1,0:T(8,128)(2,1)S(1)}, f32[3,1024,768]{2,1,0:T(8,128)}) fusion(f32[3,1024,768]{2,1,0:T(8,128)S(1)} %get-tuple-element.172, f32[768]{0:T(1024)S(1)} %copy-done.43, u8[1024,768]{1,0:T(8,128)(4,1)S(1)} %get-tuple-element.109, u8[1024,768]{1,0:T(8,128)(4,1)S(1)} %get-tuple-element.108), kind=kLoop, calls=%fused_computation.70 | loop fusion | flops 167510016 | bytes 25168896 | tf_op jit(solution)/shard_map/convert_element_type | solution.py:92
  236.5 7.9 %bitcast_convert_fusion.2 = bf16[768,576]{0,1:T(8,128)(2,1)} fusion(bf16[3,1024,576]{1,2,0:T(8,128)(2,1)S(1)} %bitcast.224, bf16[3,1024,768]{2,1,0:T(8,128)(2,1)} %all-gather.3.cloned.1.call-done), kind=kOutput, calls=%fused_computation.125 | convolution fusion | flops 2718351360 | bytes 9142272 | tf_op jit(solution)/shard_map/bsd,bsc->dc/dot_general | solution.py:130
  244.4 4.6 fusion.74
  249.0 14.2 %fusion.98 = (bf16[768]{0:T(1024)(128)(2,1)S(1)}, bf16[3,1024,768]{2,1,0:T(8,128)(2,1)}) fusion(f32[3,1024,768]{2,1,0:T(8,128)} %get-tuple-element.160, bf16[3,1024,768]{2,1,0:T(8,128)(2,1)} %all-gather.5.cloned.1.call-done, bf16[768,768]{1,0:T(8,128)(2,1)S(1)} %copy-done.44, f32[3,1024,768]{2,1,0:T(8,128)S(1)} %get-tuple-element.172, f32[768]{0:T(1024)S(1)} %copy-done.43), kind=kOutput, calls=%fused_computation.165 | convolution fusion | flops 3661626624 | bytes 29495808 | tf_op jit(solution)/shard_map/bsd,fd->bsf/dot_general | solution.py:104
  263.2 8.7 %bitcast_convert_fusion.1 = bf16[768,768]{1,0:T(8,128)(2,1)} fusion(bf16[3,1024,768]{2,1,0:T(8,128)(2,1)} %all-gather.3.cloned.1.call-done, bf16[3,1024,768]{2,1,0:T(8,128)(2,1)} %get-tuple-element.174), kind=kOutput, calls=%fused_computation.108 | convolution fusion | flops 3624468480 | bytes 10616832 | tf_op jit(solution)/shard_map/bsd,bsf->df/dot_general | solution.py:107
  271.9 7.3 %bitcast_convert_fusion = bf16[768,768]{1,0:T(8,128)(2,1)} fusion(bf16[3,1024,768]{2,1,0:T(8,128)(2,1)S(1)} %get-tuple-element.159, bf16[3,1024,768]{2,1,0:T(8,128)(2,1)} %all-gather.5.cloned.1.call-done), kind=kOutput, calls=%fused_computation.107 | convolution fusion | flops 3624468480 | bytes 10616832 | tf_op jit(solution)/shard_map/bsf,bsd->fd/dot_general | solution.py:102
  279.3 5.9 %fusion.81 = f32[3,1024,768]{2,1,0:T(8,128)S(1)} fusion(bf16[3,1024,768]{2,1,0:T(8,128)(2,1)} %get-tuple-element.174, bf16[768,768]{1,0:T(8,128)(2,1)S(1)} %copy-done), kind=kOutput, calls=%fused_computation.136 | convolution fusion | flops 3623878656 | bytes 15335424 | tf_op jit(solution)/shard_map/bsf,df->bsd/dot_general | solution.py:109
  285.3 5.6 add_convert_fusion
  291.0 6.1 %fusion.79 = f32[3,1024,768]{2,1,0:T(8,128)S(1)} fusion(bf16[3,1024,768]{2,1,0:T(8,128)(2,1)} %copy-done.13, bf16[768,768]{1,0:T(8,128)(2,1)S(1)} %copy-done.44), kind=kOutput, calls=%fused_computation.134 | convolution fusion | flops 3623878656 | bytes 15335424 | tf_op jit(solution)/shard_map/bsf,fd->bsd/dot_general | solution.py:94
  297.1 4.9 add_convert_fusion.2
  302.0 22.5 %all-reduce.1 = (bf16[3,64]{1,0:T(4,128)(2,1)S(1)}, bf16[3,64]{1,0:T(4,128)(2,1)S(1)}, bf16[768]{0:T(1024)(128)(2,1)S(1)}) all-reduce(bf16[3,64]{1,0:T(4,128)(2,1)S(1)} %get-tuple-element.176, bf16[3,64]{1,0:T(4,128)(2,1)S(1)} %get-tuple-element.110, bf16[768]{0:T(1024)(128)(2,1)S(1)} %get-tuple-element.173), channel_id=1, replica_groups=mesh['tp'=4,'dp'=8] {'dp'}, use_global_device_ids=true, to_apply=%region_25.26 | all-reduce | flops 1152 | bytes 4608 | tf_op jit(solution)/shard_map/psum | solution.py:144
  326.3 92.2 %all-reduce.5.cloned.1.call-done = (bf16[768,576]{0,1:T(8,128)(2,1)}, bf16[192,768]{1,0:T(8,128)(2,1)}, bf16[768,768]{1,0:T(8,128)(2,1)}, bf16[768,768]{1,0:T(8,128)(2,1)}) async-done(((bf16[768,576]{0,1:T(8,128)(2,1)}, bf16[192,768]{1,0:T(8,128)(2,1)}, bf16[768,768]{1,0:T(8,128)(2,1)}, bf16[768,768]{1,0:T(8,128)(2,1)}), (bf16[768,576]{0,1:T(8,128)(2,1)}, bf16[192,768]{1,0:T(8,128)(2,1)}, ...) | async-done | bytes 3538960 | tf_op jit(solution)/shard_map/psum | solution.py:143
  418.5 2.9 convert_element_type.130
  421.5 1.6 convert_element_type.133
  423.1 1.3 convert_element_type.122
  424.4 0.9 convert_element_type.128
  425.3 42.6 %reduce-scatter.5.cloned.1.call-done = bf16[3,256,768]{2,1,0:T(8,128)(2,1)} async-done(((bf16[3,1024,768]{2,1,0:T(8,128)(2,1)}), bf16[3,256,768]{2,1,0:T(8,128)(2,1)}) %reduce-scatter.5.cloned.1.call-update) | async-done | bytes 1179664 | tf_op jit(solution)/shard_map/reduce_scatter | solution.py:134
  467.8 2.0 fusion.68
  470.6 1.9 fusion.66
  473.1 45.0 %reduce-scatter.3.cloned.1.call-done = bf16[3,256,768]{2,1,0:T(8,128)(2,1)} async-done(((bf16[3,1024,768]{2,1,0:T(8,128)(2,1)}), bf16[3,256,768]{2,1,0:T(8,128)(2,1)}) %reduce-scatter.3.cloned.1.call-update) | async-done | bytes 1179664 | tf_op jit(solution)/shard_map/reduce_scatter | solution.py:97
  518.1 4.5 convert_reduce_fusion.1
  522.6 39.6 %all-reduce = (f32[768]{0:T(1024)}, f32[768]{0:T(1024)}) all-reduce(f32[768]{0:T(1024)} %get-tuple-element.114, f32[768]{0:T(1024)} %get-tuple-element.169), channel_id=1, replica_groups=mesh['tp'=4,'dp'=8] {'tp','dp'}, use_global_device_ids=true, to_apply=%region_22.23 | all-reduce | flops 1536 | bytes 12288 | tf_op jit(solution)/shard_map/psum | solution.py:141
  (163 shorter events, 25.8 us)
Async XLA Ops:
  7.2 199.6 %copy-start = (bf16[768,768]{1,0:T(8,128)(2,1)S(1)}, bf16[768,768]{1,0:T(8,128)(2,1)}, u32[]{:S(2)}) copy-start(bf16[768,768]{1,0:T(8,128)(2,1)} %param.23) | copy-start | bytes 3538948
  7.2 4.7 copy-start.6
  7.2 4.7 copy-start.34
  7.2 46.4 %all-gather.3.cloned.1.call-start = ((), (), s32[]{:S(2)}) async-start(), calls=%async_computation.2 | async-start | bytes 5898240 | tf_op jit(solution)/shard_map/all_gather | solution.py:76
  8.9 2.4 copy-start.32
  10.7 0.6 copy-start.38
  11.3 0.6 copy-start.36
  13.3 40.3 %copy-start.45 = (bf16[768,576]{0,1:T(8,128)(2,1)S(1)}, bf16[768,576]{0,1:T(8,128)(2,1)}, u32[]{:S(2)}) copy-start(bf16[768,576]{0,1:T(8,128)(2,1)} %param.19) | copy-start | bytes 2654212
  13.3 88.3 %all-gather.5.cloned.1.call-start = ((), (), s32[]{:S(2)}) async-start(), calls=%async_computation.4 | async-start | bytes 5898240 | tf_op jit(solution)/shard_map/all_gather | solution.py:101
  14.1 404.4 %all-reduce.5.cloned.1.call-start = ((), (), s32[]{:S(2)}) async-start(), calls=%async_computation.6 | async-start | bytes 7077888 | tf_op jit(solution)/shard_map/psum | solution.py:143
  59.2 4.0 copy-start.2
  59.2 4.5 copy-start.4
  60.9 2.3 copy-start.16
  61.3 0.6 copy-start.26
  61.3 1.9 copy-start.22
  61.9 1.4 copy-start.41
  62.2 1.5 copy-start.18
  62.6 0.6 copy-start.28
  63.2 0.7 copy-start.39
  63.2 1.1 copy-start.24
  63.9 0.7 copy-start.47
  101.6 6.0 %copy-start.8 = (bf16[3,1024,3,64]{1,3,2,0:T(8,128)(2,1)}, bf16[3,1024,3,64]{1,3,2,0:T(8,128)(2,1)S(1)}, u32[]{:S(2)}) copy-start(bf16[3,1024,3,64]{1,3,2,0:T(8,128)(2,1)S(1)} %get-tuple-element.394) | copy-start | bytes 3538948
  101.6 6.0 %copy-start.9 = (bf16[3,1024,3,64]{1,3,2,0:T(8,128)(2,1)}, bf16[3,1024,3,64]{1,3,2,0:T(8,128)(2,1)S(1)}, u32[]{:S(2)}) copy-start(bf16[3,1024,3,64]{1,3,2,0:T(8,128)(2,1)S(1)} %get-tuple-element.395) | copy-start | bytes 3538948
  107.6 87.6 %copy-start.5 = (f32[3,1024,3,1,64]{1,4,3,2,0:T(8,128)S(1)}, f32[3,1024,3,1,64]{1,4,3,2,0:T(8,128)}, u32[]{:S(2)}) copy-start(f32[3,1024,3,1,64]{1,4,3,2,0:T(8,128)} %copy-done.4) | copy-start | bytes 7077892
  107.6 87.6 %copy-start.40 = (f32[3,64]{1,0:T(4,128)S(1)}, f32[3,64]{1,0:T(4,128)}, u32[]{:S(2)}) copy-start(f32[3,64]{1,0:T(4,128)} %param.20) | copy-start | bytes 2308
  123.3 6.0 %copy-start.1 = (bf16[3,1024,1024]{1,2,0:T(8,128)(2,1)S(1)}, bf16[3,1024,1024]{1,2,0:T(8,128)(2,1)}, u32[]{:S(2)}) copy-start(bf16[3,1024,1024]{1,2,0:T(8,128)(2,1)} %multiply_convert_fusion.6) | copy-start | bytes 18874372 | tf_op jit(solution)/shard_map/while
  152.4 6.0 %copy-start.1 = (bf16[3,1024,1024]{1,2,0:T(8,128)(2,1)S(1)}, bf16[3,1024,1024]{1,2,0:T(8,128)(2,1)}, u32[]{:S(2)}) copy-start(bf16[3,1024,1024]{1,2,0:T(8,128)(2,1)} %multiply_convert_fusion.6) | copy-start | bytes 18874372 | tf_op jit(solution)/shard_map/while
  181.5 6.0 %copy-start.1 = (bf16[3,1024,1024]{1,2,0:T(8,128)(2,1)S(1)}, bf16[3,1024,1024]{1,2,0:T(8,128)(2,1)}, u32[]{:S(2)}) copy-start(bf16[3,1024,1024]{1,2,0:T(8,128)(2,1)} %multiply_convert_fusion.6) | copy-start | bytes 18874372 | tf_op jit(solution)/shard_map/while
  195.2 2.6 copy-start.29
  195.2 2.6 copy-start.3
  195.2 3.1 copy-start.11
  195.2 3.1 copy-start.17
  195.2 3.1 copy-start.42
  198.3 0.8 copy-start.27
  198.3 1.7 copy-start.10
  198.3 1.7 copy-start.19
  198.3 1.7 copy-start.23
  198.4 1.7 copy-start.25
  203.6 3.1 slice-start
  204.4 2.3 slice-start.1
  206.4 0.7 copy-start.43
  207.1 29.4 %copy-start.14 = (bf16[3,1024,3,3,64]{1,4,3,2,0:T(8,128)(2,1)}, bf16[3,1024,3,3,64]{1,4,3,2,0:T(8,128)(2,1)S(1)}, u32[]{:S(2)}) copy-start(bf16[3,1024,3,3,64]{1,4,3,2,0:T(8,128)(2,1)S(1)} %copy.30) | copy-start | bytes 10616836
  236.5 35.4 %copy-start.13 = (bf16[3,1024,768]{2,1,0:T(8,128)(2,1)}, bf16[3,1024,768]{2,1,0:T(8,128)(2,1)S(1)}, u32[]{:S(2)}) copy-start(bf16[3,1024,768]{2,1,0:T(8,128)(2,1)S(1)} %get-tuple-element.159) | copy-start | bytes 14155780
  244.4 4.6 copy-start.44
  279.2 6.0 %copy-start.46 = (bf16[768,576]{0,1:T(8,128)(2,1)S(1)}, bf16[768,576]{0,1:T(8,128)(2,1)}, u32[]{:S(2)}) copy-start(bf16[768,576]{0,1:T(8,128)(2,1)} %param.19) | copy-start | bytes 2654212
  279.3 188.6 %reduce-scatter.5.cloned.1.call-start = ((), (), s32[]{:S(2)}) async-start(), calls=%async_computation.5 | async-start | bytes 5898240 | tf_op jit(solution)/shard_map/reduce_scatter | solution.py:134
  279.3 6.0 %copy-start.15 = (bf16[3,1024,3,3,64]{1,4,3,2,0:T(8,128)(2,1)S(1)}, bf16[3,1024,3,3,64]{1,4,3,2,0:T(8,128)(2,1)}, u32[]{:S(2)}) copy-start(bf16[3,1024,3,3,64]{1,4,3,2,0:T(8,128)(2,1)} %copy-done.14) | copy-start | bytes 10616836
  290.9 6.1 %copy-start.31 = (bf16[192,768]{1,0:T(8,128)(2,1)S(1)}, bf16[192,768]{1,0:T(8,128)(2,1)}, u32[]{:S(2)}) copy-start(bf16[192,768]{1,0:T(8,128)(2,1)} %param.22) | copy-start | bytes 884740
  291.0 227.1 %reduce-scatter.3.cloned.1.call-start = ((), (), s32[]{:S(2)}) async-start(), calls=%async_computation.3 | async-start | bytes 5898240 | tf_op jit(solution)/shard_map/reduce_scatter | solution.py:97
  418.5 2.9 copy-start.20
  421.5 1.6 copy-start.21
  421.5 2.9 copy-start.30
  423.0 44.8 %copy-start.7 = (bf16[3,256,768]{2,1,0:T(8,128)(2,1)S(1)}, bf16[3,256,768]{2,1,0:T(8,128)(2,1)}, u32[]{:S(2)}) copy-start(bf16[3,256,768]{2,1,0:T(8,128)(2,1)} %param.16) | copy-start | bytes 3538948
  423.0 44.8 %copy-start.33 = (f32[3,256]{1,0:T(4,128)S(1)}, f32[3,256]{1,0:T(4,128)}, u32[]{:S(2)}) copy-start(f32[3,256]{1,0:T(4,128)} %copy-done.32) | copy-start | bytes 9220
  423.1 44.8 %copy-start.35 = (f32[768]{0:T(1024)S(1)}, f32[768]{0:T(1024)}, u32[]{:S(2)}) copy-start(f32[768]{0:T(1024)} %param.18) | copy-start | bytes 9220
  423.1 47.5 %copy-start.37 = (f32[3,256]{1,0:T(4,128)S(1)}, f32[3,256]{1,0:T(4,128)}, u32[]{:S(2)}) copy-start(f32[3,256]{1,0:T(4,128)} %copy-done.36) | copy-start | bytes 9220
  467.8 2.7 copy-start.12
Sparse Core Ops, SparseCore 0:
  13.5 40.1 all-gather.2
  55.2 37.4 all-gather.4
  279.4 139.1 all-reduce.4
  420.9 46.8 reduce-scatter.4
  470.2 47.8 reduce-scatter.2
where the time goes:
time: 580 us; the launch traced here: 569 us
  waiting for transfers between devices  216 us (37%)
  matrix products  169 us (29%)
  other arithmetic  91.3 us (16%)
  blocking collectives  62.1 us (11%)
  local copies, waits for them, and re-layouts  15.1 us (3%)
  between operations  14.8 us (3%)
    psum x1, waiting for transfers between devices, shards(): lax.psum(d_qkv.astype(jnp.bfloat16), 'dp').astype(jnp.float32)  92.2 us
    reduce_scatter x1, waiting for transfers between devices, shards(): lax.psum_scatter(partial_sum.astype(jnp.bfloat16), 'tp', scatter_dimensio...  45 us
    reduce_scatter x1, waiting for transfers between devices, shards(): lax.psum_scatter(d_normed.astype(jnp.bfloat16), 'tp', scatter_dimension=1...  42.6 us
    psum x1, blocking collectives, shards(): d_ln_gain, d_bias_two = lax.psum((d_ln_gain, d_bias_two), ('tp', 'dp'))  39.6 us
    all_gather x1, waiting for transfers between devices, shards(): normed = lax.all_gather(normed_local, 'tp', axis=1, tiled=True)  36 us
    convert_element_type x1, other arithmetic, shards(): active = gelu_exact(hidden).astype(jnp.bfloat16)  23 us
    psum x1, blocking collectives, shards(): lax.psum(d_q_gain.astype(jnp.bfloat16), 'dp').astype(jnp.float32)  22.5 us
    dot_general x3, matrix products, backward_keys(): jnp.einsum('hqk,qhd->khd', d_scores, queries, preferred_element_type=jnp....  17.9 us
  transfers between devices with their start and end apart: 5, of which 4 were waited for; matrix products, arithmetic and copies ran while one was open for 15% of the time, Pallas kernels for 0%

commit v1 on v0

--- a/solution.py
+++ b/solution.py
@@ -73,7 +73,14 @@
     factor = head_size ** (-0.5)
     tokens_float = tokens.astype(jnp.float32)
     normed_local = layer_norm(tokens_float, ln_gain).astype(jnp.bfloat16)
-    normed = lax.all_gather(normed_local, "tp", axis=1, tiled=True)
+    ways, here, step = (lax.axis_size("tp"), lax.axis_index("tp"), normed_local.shape[1])
+    line, have = (normed_local, 1)
+    while have < ways:
+        line = jnp.concatenate(
+            [line, lax.ppermute(line, "tp", [(d, (d - have) % ways) for d in range(ways)])], axis=1
+        )
+        have = 2 * have
+    normed = jnp.roll(line, here * step, axis=1)
     seq_len = normed.shape[1]
     joined = jnp.einsum("bsd,dc->bsc", normed, w_qkv, preferred_element_type=jnp.float32)
     split_heads = joined.reshape(images, seq_len, heads_here, 3, head_size)

time: 580 us -> 650 us (1.12)
  waiting for transfers between devices: 216 us -> 268 us
  local copies, waits for them, and re-layouts: 15.1 us -> 26.8 us
    ppermute x0 -> x2, waiting for transfers between devices: none -> 88 us  [shards(): lax.ppermute(line, 'tp', [(d, (d - have) % ways) for d in range(ways)])]
    all_gather x1 -> x0, waiting for transfers between devices: 36 us -> none  [shards(): normed = lax.all_gather(normed_local, 'tp', axis=1, tiled=True)]
    unnamed x99 -> x111, local copies, waits for them, and re-layouts: 7 us -> 15.2 us
  transfers between devices with their start and end apart: 5 -> 6, of which waited for: 4 -> 5; matrix products, arithmetic and copies ran while one was open for 15% -> 20% of each run, Pallas kernels for 0% -> 0%
where the time goes in v1:
time: 650 us; the launch traced here: 639 us
  waiting for transfers between devices  268 us (41%)
  matrix products  170 us (26%)
  other arithmetic  93.1 us (14%)
  blocking collectives  62.5 us (10%)
  local copies, waits for them, and re-layouts  26.8 us (4%)
  between operations  15 us (2%)
    psum x1, waiting for transfers between devices, shards(): lax.psum(d_qkv.astype(jnp.bfloat16), 'dp').astype(jnp.float32)  92.1 us
    ppermute x2, waiting for transfers between devices, shards(): lax.ppermute(line, 'tp', [(d, (d - have) % ways) for d in range(ways)])  88 us
    reduce_scatter x1, waiting for transfers between devices, shards(): lax.psum_scatter(partial_sum.astype(jnp.bfloat16), 'tp', scatter_dimensio...  45 us
    reduce_scatter x1, waiting for transfers between devices, shards(): lax.psum_scatter(d_normed.astype(jnp.bfloat16), 'tp', scatter_dimension=1...  42.7 us
    psum x1, blocking collectives, shards(): d_ln_gain, d_bias_two = lax.psum((d_ln_gain, d_bias_two), ('tp', 'dp'))  39.6 us
    psum x1, blocking collectives, shards(): lax.psum(d_q_gain.astype(jnp.bfloat16), 'dp').astype(jnp.float32)  22.9 us
    convert_element_type x1, other arithmetic, shards(): active = gelu_exact(hidden).astype(jnp.bfloat16)  22.8 us
    dot_general x3, matrix products, backward_keys(): jnp.einsum('hqk,qhd->khd', d_scores, queries, preferred_element_type=jnp....  17.9 us
  transfers between devices with their start and end apart: 6, of which 5 were waited for; matrix products, arithmetic and copies ran while one was open for 20% of the time, Pallas kernels for 0%

profile of v1, /device:TPU:0, one launch (start us, length us, event | category | flops | bytes accessed | tf_op | source)
XLA Modules:
  0.0 639.0 jit_solution(5633780048686822125)
XLA Ops:
  7.2 1.6 convert_reduce_fusion
  8.9 1.7 fusion.75
  11.3 2.2 constant_dynamic-update-slice_fusion.5
  13.4 2.4 collective-permute-start
  15.9 13.7 %collective-permute-done = bf16[3,256,768]{2,1,0:T(8,128)(2,1)S(1)} collective-permute-done((bf16[3,256,768]{2,1,0:T(8,128)(2,1)S(1)}, bf16[3,256,768]{2,1,0:T(8,128)(2,1)S(1)}, u32[]{:S(2)}, u32[]{:S(2)}) %collective-permute-start) | collective-permute-done | bytes 1179680 | tf_op jit(solution)/shard_map/ppermute | solution.py:80
  33.0 2.4 copy.88
  36.5 74.2 %collective-permute-done.1 = bf16[3,512,768]{2,1,0:T(8,128)(2,1)} collective-permute-done((bf16[3,512,768]{2,1,0:T(8,128)(2,1)}, bf16[3,512,768]{2,1,0:T(8,128)(2,1)}, u32[]{:S(2)}, u32[]{:S(2)}) %collective-permute-start.1) | collective-permute-done | bytes 2359328 | tf_op jit(solution)/shard_map/ppermute | solution.py:80
  110.8 3.2 constant_dynamic-update-slice_fusion.3
  116.2 3.2 constant_dynamic-update-slice_fusion
  119.4 4.8 fusion.69
  129.8 37.1 %while.28 = (s32[]{:T(128)}, bf16[3,1024,3,64]{1,3,2,0:T(8,128)(2,1)}, f32[3,3,1024]{2,1,0:T(4,128)}, bf16[3,1024,3,64]{1,3,2,0:T(8,128)(2,1)}, s32[3]{0:T(128)S...) while((s32[]{:T(128)}, bf16[3,1024,3,64]{1,3,2,0:T(8,128)(2,1)}, ...), condition=%wide.region_9.10_spmd.clone, body=%wide.region_6.9_spmd.sunk.clone | while | flops 843053056 | bytes 39823964 | solution.py:96
  131.0 2.4 fusion.162
  133.4 3.2 fusion.163
  137.2 4.9 fusion.164
  143.4 2.4 fusion.162
  145.7 3.2 fusion.163
  149.5 4.9 fusion.164
  155.7 2.4 fusion.162
  158.1 3.2 fusion.163
  161.9 4.9 fusion.164
  166.9 9.1 %fusion.80 = (u8[1024,768]{1,0:T(8,128)(4,1)S(1)}, u8[1024,768]{1,0:T(8,128)(4,1)S(1)}, f32[3,1024,768]{2,1,0:T(8,128)S(1)}) fusion(f32[768]{0:T(1024)S(1)} %copy-done.43, bf16[768,768]{1,0:T(8,128)(2,1)S(1)} %copy-done, bf16[3,2048,768]{2,1,0:T(8,128)(2,1)} %constant_dynamic-update-slice_fusion, s32[]{:T(128)S(6)} %select_n.21), kind=kOutput, calls=%fused_computation.131 | convolution fusion | flops 3655335936 | bytes 16911364 | tf_op jit(solution)/shard_map/bsd,df->bsf/dot_general | solution.py:98
  176.0 3.7 copy-done.13
  179.6 22.8 %multiply_convert_fusion.1 = (bf16[3,1024,768]{2,1,0:T(8,128)(2,1)}, f32[3,1024,768]{2,1,0:T(8,128)}) fusion(f32[3,1024,768]{2,1,0:T(8,128)S(1)} %get-tuple-element.174, f32[768]{0:T(1024)S(1)} %copy-done.43, u8[1024,768]{1,0:T(8,128)(4,1)S(1)} %get-tuple-element.109, u8[1024,768]{1,0:T(8,128)(4,1)S(1)} %get-tuple-element.108), kind=kLoop, calls=%fused_computation.70 | loop fusion | flops 167510016 | bytes 25168896 | tf_op jit(solution)/shard_map/convert_element_type | solution.py:99
  202.5 5.0 convolution_convert_fusion
  207.5 87.7 %while.29 = (s32[]{:T(128)}, f32[3,1024,3,64]{1,3,2,0:T(8,128)}, f32[3,1024,3,64]{1,3,2,0:T(8,128)}, bf16[3,1024,3,64]{1,3,2,0:T(8,128)(2,1)}, bf16[3,1024,3,64]...) while((s32[]{:T(128)}, f32[3,1024,3,64]{1,3,2,0:T(8,128)}, ...), condition=%wide.region_13.14_spmd.clone, body=%wide.region_11.13_spmd.sunk.clone | while | flops 2060843008 | bytes 124744848 | solution.py:125
  207.5 3.1 fusion.173
  212.6 4.8 multiply_reduce_fusion.9
  217.4 5.7 multiply_convert_fusion.6
  223.2 6.0 fusion.175
  229.1 3.1 fusion.174
  232.2 4.6 fusion.176
  236.8 2.9 fusion.173
  241.8 4.8 multiply_reduce_fusion.9
  246.6 5.7 multiply_convert_fusion.6
  252.3 6.0 fusion.175
  258.3 3.1 fusion.174
  261.4 4.6 fusion.176
  266.0 2.9 fusion.173
  270.9 4.8 multiply_reduce_fusion.9
  275.8 5.7 multiply_convert_fusion.6
  281.5 6.0 fusion.175
  287.5 3.1 fusion.174
  290.6 4.6 fusion.176
  295.3 2.5 multiply_reduce_fusion.4
  299.6 2.6 multiply_reduce_fusion.1
  306.0 7.8 %bitcast_convert_fusion.2 = bf16[768,576]{0,1:T(8,128)(2,1)} fusion(bf16[3,1024,576]{1,2,0:T(8,128)(2,1)S(1)} %bitcast.224, bf16[3,2048,768]{2,1,0:T(8,128)(2,1)} %constant_dynamic-update-slice_fusion, s32[]{:T(128)S(6)} %select_n.21), kind=kOutput, calls=%fused_computation.134 | convolution fusion | flops 2718351360 | bytes 9142276 | tf_op jit(solution)/shard_map/bsd,bsc->dc/dot_general | solution.py:137
  313.8 14.2 %fusion.113 = (bf16[768]{0:T(1024)(128)(2,1)S(1)}, bf16[3,1024,768]{2,1,0:T(8,128)(2,1)}) fusion(f32[3,1024,768]{2,1,0:T(8,128)} %get-tuple-element.160, bf16[3,1024,768]{2,1,0:T(8,128)(2,1)} %all-gather.2.cloned.1.call-done, bf16[768,768]{1,0:T(8,128)(2,1)S(1)} %copy-done.45, f32[3,1024,768]{2,1,0:T(8,128)S(1)} %bitcast.219, f32[768]{0:T(1024)S(1)} %copy-done.44), kind=kOutput, calls=%fused_computation.182 | convolution fusion | flops 3661626624 | bytes 29495808 | tf_op jit(solution)/shard_map/bsd,fd->bsf/dot_general | solution.py:111
  328.0 8.7 %bitcast_convert_fusion.1 = bf16[768,768]{1,0:T(8,128)(2,1)} fusion(bf16[3,1024,768]{2,1,0:T(8,128)(2,1)} %get-tuple-element.176, bf16[3,2048,768]{2,1,0:T(8,128)(2,1)} %constant_dynamic-update-slice_fusion, s32[]{:T(128)S(6)} %select_n.21), kind=kOutput, calls=%fused_computation.117 | convolution fusion | flops 3624468480 | bytes 10616836 | tf_op jit(solution)/shard_map/bsd,bsf->df/dot_general | solution.py:114
  336.7 4.5 fusion.86
  341.2 7.3 %bitcast_convert_fusion = bf16[768,768]{1,0:T(8,128)(2,1)} fusion(bf16[3,1024,768]{2,1,0:T(8,128)(2,1)S(1)} %bitcast.223, bf16[3,1024,768]{2,1,0:T(8,128)(2,1)} %all-gather.2.cloned.1.call-done), kind=kOutput, calls=%fused_computation.116 | convolution fusion | flops 3624468480 | bytes 10616832 | tf_op jit(solution)/shard_map/bsf,bsd->fd/dot_general | solution.py:109
  348.6 5.9 fusion.93
  354.6 5.6 add_convert_fusion
  360.6 5.8 fusion.91
  366.4 5.0 add_convert_fusion.2
  371.4 22.9 %all-reduce.1 = (bf16[3,64]{1,0:T(4,128)(2,1)S(1)}, bf16[3,64]{1,0:T(4,128)(2,1)S(1)}, bf16[768]{0:T(1024)(128)(2,1)S(1)}) all-reduce(bf16[3,64]{1,0:T(4,128)(2,1)S(1)} %get-tuple-element.178, bf16[3,64]{1,0:T(4,128)(2,1)S(1)} %get-tuple-element.110, bf16[768]{0:T(1024)(128)(2,1)S(1)} %get-tuple-element.175), channel_id=1, replica_groups=mesh['tp'=4,'dp'=8] {'dp'}, use_global_device_ids=true, to_apply=%region_25.26 | all-reduce | flops 1152 | bytes 4608 | tf_op jit(solution)/shard_map/psum | solution.py:151
  396.0 92.1 %all-reduce.5.cloned.1.call-done = (bf16[768,576]{0,1:T(8,128)(2,1)}, bf16[192,768]{1,0:T(8,128)(2,1)}, bf16[768,768]{1,0:T(8,128)(2,1)}, bf16[768,768]{1,0:T(8,128)(2,1)}) async-done(((bf16[768,576]{0,1:T(8,128)(2,1)}, bf16[192,768]{1,0:T(8,128)(2,1)}, bf16[768,768]{1,0:T(8,128)(2,1)}, bf16[768,768]{1,0:T(8,128)(2,1)}), (bf16[768,576]{0,1:T(8,128)(2,1)}, bf16[192,768]{1,0:T(8,128)(2,1)}, ...) | async-done | bytes 3538960 | tf_op jit(solution)/shard_map/psum | solution.py:150
  488.2 3.0 convert_element_type.130
  491.2 1.6 convert_element_type.133
  495.0 42.7 %reduce-scatter.5.cloned.1.call-done = bf16[3,256,768]{2,1,0:T(8,128)(2,1)} async-done(((bf16[3,1024,768]{2,1,0:T(8,128)(2,1)}), bf16[3,256,768]{2,1,0:T(8,128)(2,1)}) %reduce-scatter.5.cloned.1.call-update) | async-done | bytes 1179664 | tf_op jit(solution)/shard_map/reduce_scatter | solution.py:141
  537.7 2.0 fusion.76
  540.4 1.9 fusion.74
  542.9 45.0 %reduce-scatter.3.cloned.1.call-done = bf16[3,256,768]{2,1,0:T(8,128)(2,1)} async-done(((bf16[3,1024,768]{2,1,0:T(8,128)(2,1)}), bf16[3,256,768]{2,1,0:T(8,128)(2,1)}) %reduce-scatter.3.cloned.1.call-update) | async-done | bytes 1179664 | tf_op jit(solution)/shard_map/reduce_scatter | solution.py:104
  587.9 4.5 convert_reduce_fusion.1
  592.4 39.6 %all-reduce = (f32[768]{0:T(1024)}, f32[768]{0:T(1024)}) all-reduce(f32[768]{0:T(1024)} %get-tuple-element.114, f32[768]{0:T(1024)} %get-tuple-element.171), channel_id=1, replica_groups=mesh['tp'=4,'dp'=8] {'tp','dp'}, use_global_device_ids=true, to_apply=%region_22.23 | all-reduce | flops 1536 | bytes 12288 | tf_op jit(solution)/shard_map/psum | solution.py:148
  (179 shorter events, 35.2 us)
Async XLA Ops:
  7.2 159.7 %copy-start = (bf16[768,768]{1,0:T(8,128)(2,1)S(1)}, bf16[768,768]{1,0:T(8,128)(2,1)}, u32[]{:S(2)}) copy-start(bf16[768,768]{1,0:T(8,128)(2,1)} %param.23) | copy-start | bytes 3538948
  7.2 4.1 copy-start.6
  7.2 195.3 %all-gather.2.cloned.1.call-start = ((), (), s32[]{:S(2)}) async-start(), calls=%async_computation.3 | async-start | bytes 5898240 | tf_op jit(solution)/shard_map/all_gather | solution.py:108
  8.9 4.5 copy-start.33
  10.7 0.6 copy-start.38
  11.3 4.6 copy-start.36
  13.4 16.2 %collective-permute-start = (bf16[3,256,768]{2,1,0:T(8,128)(2,1)S(1)}, bf16[3,256,768]{2,1,0:T(8,128)(2,1)S(1)}, u32[]{:S(2)}, u32[]{:S(2)}) collective-permute-start(bf16[3,256,768]{2,1,0:T(8,128)(2,1)S(1)} %get-tuple-element.162), channel_id=1, source_target_pairs={{0,24},{8,0},{16,8},{24,16},{1,25},{9,1},{17,9},{25,17},{2,26},{10... | collective-permute-start | bytes 3538952 | tf_op jit(solution)/shard_map/ppermute | solution.py:80
  31.2 79.6 %collective-permute-start.1 = (bf16[3,512,768]{2,1,0:T(8,128)(2,1)}, bf16[3,512,768]{2,1,0:T(8,128)(2,1)}, u32[]{:S(2)}, u32[]{:S(2)}) collective-permute-start(bf16[3,512,768]{2,1,0:T(8,128)(2,1)} %pad_maximum_fusion.1), channel_id=1, source_target_pairs={{0,16},{8,24},{16,0},{24,8},{1,17},{9,25},{17,1},{25,9},{2,18},{10... | collective-permute-start | bytes 7077896 | tf_op jit(solution)/shard_map/ppermute | solution.py:80
  31.8 456.4 %all-reduce.5.cloned.1.call-start = ((), (), s32[]{:S(2)}) async-start(), calls=%async_computation.5 | async-start | bytes 7077888 | tf_op jit(solution)/shard_map/psum | solution.py:150
  115.1 4.4 copy-start.46
  125.0 3.7 copy-start.4
  125.0 4.2 copy-start.2
  126.7 2.0 copy-start.18
  127.1 0.6 copy-start.26
  127.1 1.6 copy-start.39
  127.2 2.1 copy-start.24
  127.5 1.8 copy-start.41
  127.7 2.0 copy-start.16
  128.1 0.6 copy-start.28
  128.8 1.0 copy-start.22
  128.8 1.0 copy-start.48
  129.7 37.1 %copy-start.43 = (f32[768]{0:T(1024)S(1)}, f32[768]{0:T(1024)}, u32[]{:S(2)}) copy-start(f32[768]{0:T(1024)} %param.24) | copy-start | bytes 9220
  166.8 9.1 %copy-start.8 = (bf16[3,1024,3,64]{1,3,2,0:T(8,128)(2,1)}, bf16[3,1024,3,64]{1,3,2,0:T(8,128)(2,1)S(1)}, u32[]{:S(2)}) copy-start(bf16[3,1024,3,64]{1,3,2,0:T(8,128)(2,1)S(1)} %get-tuple-element.395) | copy-start | bytes 3538948
  166.8 9.1 %copy-start.9 = (bf16[3,1024,3,64]{1,3,2,0:T(8,128)(2,1)}, bf16[3,1024,3,64]{1,3,2,0:T(8,128)(2,1)S(1)}, u32[]{:S(2)}) copy-start(bf16[3,1024,3,64]{1,3,2,0:T(8,128)(2,1)S(1)} %get-tuple-element.396) | copy-start | bytes 3538948
  176.0 3.7 copy-start.13
  179.6 22.9 %copy-start.31 = (bf16[192,768]{1,0:T(8,128)(2,1)S(1)}, bf16[192,768]{1,0:T(8,128)(2,1)}, u32[]{:S(2)}) copy-start(bf16[192,768]{1,0:T(8,128)(2,1)} %param.22) | copy-start | bytes 884740
  207.5 87.7 %copy-start.5 = (f32[3,1024,3,1,64]{1,4,3,2,0:T(8,128)S(1)}, f32[3,1024,3,1,64]{1,4,3,2,0:T(8,128)}, u32[]{:S(2)}) copy-start(f32[3,1024,3,1,64]{1,4,3,2,0:T(8,128)} %copy-done.4) | copy-start | bytes 7077892
  207.5 87.7 %copy-start.40 = (f32[3,64]{1,0:T(4,128)S(1)}, f32[3,64]{1,0:T(4,128)}, u32[]{:S(2)}) copy-start(f32[3,64]{1,0:T(4,128)} %param.20) | copy-start | bytes 2308
  223.2 6.0 copy-start.1
  252.3 6.0 copy-start.1
  281.5 6.0 copy-start.1
  295.2 2.6 copy-start.27
  295.2 2.7 copy-start.3
  295.2 3.1 copy-start.11
  295.2 3.1 copy-start.17
  295.2 3.1 copy-start.42
  297.8 1.3 copy-start.29
  297.8 1.8 copy-start.10
  297.8 1.8 copy-start.19
  297.8 1.8 copy-start.23
  297.8 1.8 copy-start.25
  305.3 8.4 %slice-start = ((s8[9437184]{0:T(1024)(128)(4,1)}), s8[4194304]{0:T(1024)(128)(4,1)S(1)}, s32[]{:S(2)}) async-start(s8[9437184]{0:T(1024)(128)(4,1)} %bitcast.218), calls=%async_computation.6 | async-start | bytes 8388608
  305.9 7.8 %copy-start.14 = (bf16[3,1024,3,3,64]{1,4,3,2,0:T(8,128)(2,1)}, bf16[3,1024,3,3,64]{1,4,3,2,0:T(8,128)(2,1)S(1)}, u32[]{:S(2)}) copy-start(bf16[3,1024,3,3,64]{1,4,3,2,0:T(8,128)(2,1)S(1)} %copy.30) | copy-start | bytes 10616836
  305.9 7.8 %slice-start.1 = ((s8[9437184]{0:T(1024)(128)(4,1)}), s8[4194304]{0:T(1024)(128)(4,1)S(1)}, s32[]{:S(2)}) async-start(s8[9437184]{0:T(1024)(128)(4,1)} %bitcast.218), calls=%async_computation.7 | async-start | bytes 8388608
  305.9 7.8 %slice-start.2 = ((s8[9437184]{0:T(1024)(128)(4,1)}), s8[1048576]{0:T(1024)(128)(4,1)S(1)}, s32[]{:S(2)}) async-start(s8[9437184]{0:T(1024)(128)(4,1)} %bitcast.218), calls=%async_computation.8 | async-start | bytes 2097152
  305.9 7.8 %copy-start.44 = (f32[768]{0:T(1024)S(1)}, f32[768]{0:T(1024)}, u32[]{:S(2)}) copy-start(f32[768]{0:T(1024)} %param.24) | copy-start | bytes 9220
  305.9 7.8 %copy-start.45 = (bf16[768,768]{1,0:T(8,128)(2,1)S(1)}, bf16[768,768]{1,0:T(8,128)(2,1)}, u32[]{:S(2)}) copy-start(bf16[768,768]{1,0:T(8,128)(2,1)} %param.25) | copy-start | bytes 3538948
  305.9 35.3 %slice-start.3 = ((s8[4718592]{0:T(1024)(128)(4,1)}), s8[4194304]{0:T(1024)(128)(4,1)S(1)}, s32[]{:S(2)}) async-start(s8[4718592]{0:T(1024)(128)(4,1)} %bitcast.222), calls=%async_computation.9 | async-start | bytes 8388608
  313.8 27.4 %slice-start.4 = ((s8[4718592]{0:T(1024)(128)(4,1)}), s8[524288]{0:T(1024)(128)(4,1)S(1)}, s32[]{:S(2)}) async-start(s8[4718592]{0:T(1024)(128)(4,1)} %bitcast.222), calls=%async_computation.10 | async-start | bytes 1048576
  348.6 6.0 copy-start.47
  348.6 189.1 %reduce-scatter.5.cloned.1.call-start = ((), (), s32[]{:S(2)}) async-start(), calls=%async_computation.4 | async-start | bytes 5898240 | tf_op jit(solution)/shard_map/reduce_scatter | solution.py:141
  348.6 6.0 copy-start.15
  360.3 6.1 copy-start.32
  360.3 227.7 %reduce-scatter.3.cloned.1.call-start = ((), (), s32[]{:S(2)}) async-start(), calls=%async_computation.2 | async-start | bytes 5898240 | tf_op jit(solution)/shard_map/reduce_scatter | solution.py:104
  488.2 3.0 copy-start.20
  488.2 4.6 copy-start.21
  491.2 2.9 copy-start.30
  491.2 46.5 %copy-start.7 = (bf16[3,256,768]{2,1,0:T(8,128)(2,1)S(1)}, bf16[3,256,768]{2,1,0:T(8,128)(2,1)}, u32[]{:S(2)}) copy-start(bf16[3,256,768]{2,1,0:T(8,128)(2,1)} %param.16) | copy-start | bytes 3538948
  491.2 46.5 %copy-start.34 = (f32[3,256]{1,0:T(4,128)S(1)}, f32[3,256]{1,0:T(4,128)}, u32[]{:S(2)}) copy-start(f32[3,256]{1,0:T(4,128)} %copy-done.33) | copy-start | bytes 9220
  491.2 46.5 %copy-start.35 = (f32[768]{0:T(1024)S(1)}, f32[768]{0:T(1024)}, u32[]{:S(2)}) copy-start(f32[768]{0:T(1024)} %param.18) | copy-start | bytes 9220
  492.8 47.6 %copy-start.37 = (f32[3,256]{1,0:T(4,128)S(1)}, f32[3,256]{1,0:T(4,128)}, u32[]{:S(2)}) copy-start(f32[3,256]{1,0:T(4,128)} %copy-done.36) | copy-start | bytes 9220
  537.7 2.7 copy-start.12
Sparse Core Ops, SparseCore 0:
  31.9 64.2 all-gather.1
  348.7 139.4 all-reduce.4
  490.7 46.8 reduce-scatter.4
  540.0 47.8 reduce-scatter.2
